TPU v7x, 256 devices: a whole 4x4x8 slice. The times are simulated.
256 devices in a mesh: dp: 8 (over y, x_lo), tensor: 32 (over z, x_hi, core).
Axes of the slice: x: 4 (x_hi: 2, x_lo: 2; x = x_hi * 2 + x_lo), y: 4, z: 8, core: 2. Of those that a mesh axis runs over, the one named last changes fastest.
Arguments:
- tokens: bfloat16 [2048, 3072], P('dp', 'tensor'), may hold values from -6 to 6
- buckets: int32 [2048], P('dp'), may hold values from 0 to 999
- modulation: float32 [1000, 3, 3072], P(None, None, 'tensor'), may hold values from -3 to 3
- up_weight: bfloat16 [3072, 12288], P(None, 'tensor'), may hold values from -0.109375 to 0.109375
- down_weight: bfloat16 [3072, 12288], P(None, 'tensor'), may hold values from -0.0546875 to 0.0546875
- output_cotangent: bfloat16 [2048, 3072], P('dp', 'tensor'), may hold values from -6 to 6
Outputs:
- mixed: bfloat16 [2048, 3072], P('dp', 'tensor')
- token_input_gradient: bfloat16 [2048, 3072], P('dp', 'tensor')
- grad_up: float32 [3072, 12288], P('dp', 'tensor')
- grad_down: float32 [3072, 12288], P('dp', 'tensor')
All inputs are finite; a program needn't handle non-finite values.
Results may differ from a plain program's by a relative error of at most 0.0062.
Values may be sent and summed in bfloat16 or wider, within the bound.
A program may use at most 64 MiB of HBM per device.

v0:
```python
import jax
import jax.numpy as jnp
from jax import lax
from jax.sharding import PartitionSpec as P


def gelu_tanh(value):
    return jax.nn.gelu(value, approximate=True)


def on_device(tokens, buckets, modulation, up_weight, down_weight, output_cotangent):
    local_cols = tokens.shape[1]
    model_width = local_cols * lax.axis_size("tensor")
    input_tokens = tokens.astype(jnp.float32)
    cond = jnp.take(modulation, buckets, axis=0)
    modulation_shift = cond[:, 0]
    modulation_scale = cond[:, 1]
    gate = cond[:, 2]
    total, squares = lax.psum(
        (jnp.sum(input_tokens, axis=1), jnp.sum(input_tokens * input_tokens, axis=1)), "tensor"
    )
    row_mean = total / model_width
    var = squares / model_width - row_mean * row_mean
    inverse_deviation = lax.rsqrt(var + 1e-06)
    normalized_input = (input_tokens - row_mean[:, None]) * inverse_deviation[:, None]
    hidden_input_rows = (normalized_input * (1.0 + modulation_scale) + modulation_shift).astype(
        jnp.bfloat16
    )
    full_in = lax.all_gather(hidden_input_rows, "tensor", axis=1, tiled=True)
    pre = jnp.dot(full_in, up_weight, preferred_element_type=jnp.float32)
    act = gelu_tanh(pre).astype(jnp.bfloat16)
    block = down_weight
    velocity = lax.psum_scatter(
        lax.dot_general(block, act, (((1,), (1,)), ((), ())), preferred_element_type=jnp.float32),
        "tensor",
        scatter_dimension=0,
        tiled=True,
    ).T
    mixed = (input_tokens + gate * velocity).astype(jnp.bfloat16)
    dvel = (output_cotangent.astype(jnp.float32) * gate).astype(jnp.bfloat16)
    full_dvel = lax.all_gather(dvel, "tensor", axis=1, tiled=True)
    dact = jnp.dot(full_dvel, down_weight, preferred_element_type=jnp.float32)
    pull = jax.vjp(gelu_tanh, pre)[1]
    dpre = pull(dact)[0].astype(jnp.bfloat16)
    block = up_weight
    dh = lax.psum_scatter(
        lax.dot_general(block, dpre, (((1,), (1,)), ((), ())), preferred_element_type=jnp.float32),
        "tensor",
        scatter_dimension=0,
        tiled=True,
    ).T
    normalized_input_gradient = dh * (1.0 + modulation_scale)
    first_product, second_product = lax.psum(
        (
            jnp.sum(normalized_input_gradient, axis=1),
            jnp.sum(normalized_input_gradient * normalized_input, axis=1),
        ),
        "tensor",
    )
    token_input_gradient = output_cotangent.astype(jnp.float32) + inverse_deviation[:, None] * (
        normalized_input_gradient
        - first_product[:, None] / model_width
        - normalized_input * second_product[:, None] / model_width
    )
    cols = full_in
    grad_up = lax.psum_scatter(
        lax.dot_general(cols, dpre, (((0,), (0,)), ((), ())), preferred_element_type=jnp.float32),
        "dp",
        scatter_dimension=0,
        tiled=True,
    )
    cols = full_dvel
    grad_down = lax.psum_scatter(
        lax.dot_general(cols, act, (((0,), (0,)), ((), ())), preferred_element_type=jnp.float32),
        "dp",
        scatter_dimension=0,
        tiled=True,
    )
    return (mixed, token_input_gradient.astype(jnp.bfloat16), grad_up, grad_down)


def solution(mesh):
    placed = (
        P("dp", "tensor"),
        P("dp"),
        P(None, None, "tensor"),
        P(None, "tensor"),
        P(None, "tensor"),
        P("dp", "tensor"),
    )
    return jax.shard_map(
        on_device,
        mesh=mesh,
        in_specs=placed,
        out_specs=(P("dp", "tensor"), P("dp", "tensor"), P("dp", "tensor"), P("dp", "tensor")),
        check_vma=False,
    )
```

profile of v0, /device:TPU:1, one launch (start us, length us, event | category | flops | bytes accessed | tf_op | source)
XLA Modules:
  0.0 722.3 jit_solution(3974144515244897455)
XLA Ops:
  7.2 0.0 copy-start
  7.2 0.0 all-gather.3.cloned.1.call-start
  7.2 0.8 compare_and_fusion
  8.1 0.7 compare_select_fusion
  8.8 0.9 copy.20
  9.7 0.1 convert_reduce_fusion
  9.8 2.8 copy.21
  12.6 2.6 gather_fusion
  15.2 0.3 broadcast_select_fusion
  15.5 0.3 fusion.23
  15.8 68.9 %all-reduce.1 = (f32[256]{0:T(256)S(1)}, f32[256]{0:T(256)S(1)}) all-reduce(f32[256]{0:T(256)S(1)} %get-tuple-element.19, f32[256]{0:T(256)S(1)} %get-tuple-element.18), channel_id=1, replica_groups=mesh['dp'=8,'tensor'=32] {'tensor'}, use_global_device_ids=true, to_apply=%region_3.4 | all-reduce | flops 512 | bytes 4096 | tf_op jit(solution)/shard_map/psum | solution.py:19
  84.7 0.1 fusion.14
  84.9 0.7 copy.24
  85.6 0.0 all-gather.3.cloned.1.call-update
  85.6 0.0 reduce-scatter.13.cloned.1.call-start
  85.7 78.6 %all-gather.3.cloned.1.call-done = bf16[256,3072]{0,1:T(8,128)(2,1)} async-done(((bf16[256,96]{0,1:T(8,128)(2,1)}), bf16[256,3072]{0,1:T(8,128)(2,1)}) %all-gather.3.cloned.1.call-update) | async-done | bytes 1572880 | tf_op jit(solution)/shard_map/all_gather | solution.py:29
  164.3 3.2 fusion.24
  167.5 2.7 convolution_bitcast_fusion.1
  170.2 3.5 copy.29
  173.8 0.0 reduce-scatter.13.cloned.1.call-update
  173.8 0.0 all-gather.5.cloned.1.call-start
  173.9 0.7 copy-done.2
  174.6 0.1 copy.25
  174.7 113.5 %reduce-scatter.13.cloned.1.call-done = f32[96,256]{1,0:T(8,128)} async-done(((f32[3072,256]{1,0:T(8,128)}), f32[96,256]{1,0:T(8,128)}) %reduce-scatter.13.cloned.1.call-update) | async-done | bytes 98320
  288.2 1.0 copy.30
  289.2 0.7 copy.26
  289.9 0.0 all-gather.5.cloned.1.call-update
  290.0 0.0 reduce-scatter.15.cloned.1.call-start
  290.0 84.3 %all-gather.5.cloned.1.call-done = bf16[256,3072]{0,1:T(8,128)(2,1)} async-done(((bf16[256,96]{0,1:T(8,128)(2,1)}), bf16[256,3072]{0,1:T(8,128)(2,1)}) %all-gather.5.cloned.1.call-update) | async-done | bytes 1572880 | tf_op jit(solution)/shard_map/all_gather | solution.py:41
  374.3 2.7 fusion.6
  377.1 2.7 convolution_bitcast_fusion
  379.8 3.5 copy.31
  383.3 0.0 reduce-scatter.15.cloned.1.call-update
  383.3 0.0 reduce-scatter.11.cloned.1.call-start
  383.4 4.6 fusion.22
  388.0 0.0 reduce-scatter.11.cloned.1.call-update
  388.0 0.0 reduce-scatter.9.cloned.1.call-start
  388.1 4.6 fusion.25
  392.6 0.0 reduce-scatter.9.cloned.1.call-update
  392.6 0.7 copy.27
  393.4 104.4 %reduce-scatter.15.cloned.1.call-done = f32[96,256]{1,0:T(8,128)} async-done(((f32[3072,256]{1,0:T(8,128)}), f32[96,256]{1,0:T(8,128)}) %reduce-scatter.15.cloned.1.call-update) | async-done | bytes 98320
  497.7 1.0 copy.32
  498.7 0.2 fusion.21
  499.0 72.0 %all-reduce = (f32[256]{0:T(256)S(1)}, f32[256]{0:T(256)S(1)}) all-reduce(f32[256]{0:T(256)S(1)} %get-tuple-element.17, f32[256]{0:T(256)S(1)} %get-tuple-element.16), channel_id=1, replica_groups=mesh['dp'=8,'tensor'=32] {'tensor'}, use_global_device_ids=true, to_apply=%region_9.10 | all-reduce | flops 512 | bytes 4096 | tf_op jit(solution)/shard_map/psum | solution.py:53
  571.0 0.2 fusion.8
  571.2 0.7 copy.28
  571.9 36.7 %reduce-scatter.11.cloned.1.call-done = f32[384,384]{1,0:T(8,128)} async-done(((f32[3072,384]{1,0:T(8,128)}), f32[384,384]{1,0:T(8,128)}) %reduce-scatter.11.cloned.1.call-update) | async-done | bytes 589840 | tf_op jit(solution)/shard_map/reduce_scatter | solution.py:73
  608.7 106.7 %reduce-scatter.9.cloned.1.call-done = f32[384,384]{1,0:T(8,128)} async-done(((f32[3072,384]{1,0:T(8,128)}), f32[384,384]{1,0:T(8,128)}) %reduce-scatter.9.cloned.1.call-update) | async-done | bytes 589840 | tf_op jit(solution)/shard_map/reduce_scatter | solution.py:66
  (8 shorter events, 0.1 us)
Async XLA Ops:
  7.2 160.3 %copy-start = (bf16[3072,384]{1,0:T(8,128)(2,1)S(1)}, bf16[3072,384]{1,0:T(8,128)(2,1)}, u32[]{:S(2)}) copy-start(bf16[3072,384]{1,0:T(8,128)(2,1)} %param.10) | copy-start | bytes 7077892
  7.2 157.2 %all-gather.3.cloned.1.call-start = ((), (), s32[]{:S(2)}) async-start(), calls=%async_computation.4 | async-start | bytes 1622016 | tf_op jit(solution)/shard_map/all_gather | solution.py:29
  85.6 202.5 %reduce-scatter.13.cloned.1.call-start = ((), (), s32[]{:S(2)}) async-start(), calls=%async_computation.8 | async-start | bytes 3244032
  173.8 0.8 copy-start.2
  173.8 200.5 %all-gather.5.cloned.1.call-start = ((), (), s32[]{:S(2)}) async-start(), calls=%async_computation.5 | async-start | bytes 1622016 | tf_op jit(solution)/shard_map/all_gather | solution.py:41
  290.0 207.8 %reduce-scatter.15.cloned.1.call-start = ((), (), s32[]{:S(2)}) async-start(), calls=%async_computation.9 | async-start | bytes 3244032
  374.3 2.7 copy-start.1
  383.3 225.3 %reduce-scatter.11.cloned.1.call-start = ((), (), s32[]{:S(2)}) async-start(), calls=%async_computation.7 | async-start | bytes 5308416 | tf_op jit(solution)/shard_map/reduce_scatter | solution.py:73
  388.0 327.4 %reduce-scatter.9.cloned.1.call-start = ((), (), s32[]{:S(2)}) async-start(), calls=%async_computation.6 | async-start | bytes 5308416 | tf_op jit(solution)/shard_map/reduce_scatter | solution.py:66
Sparse Core Ops, SparseCore 0:
  85.8 78.5 all-gather.2
  173.9 114.2 reduce-scatter.12
  291.6 82.7 all-gather.4
  383.5 114.2 reduce-scatter.14
  500.7 107.9 reduce-scatter.10
  611.7 103.7 reduce-scatter.8
where the time goes:
time: 723 us; the launch traced here: 722 us
  waiting for transfers between devices  524 us (72%)
  blocking collectives  141 us (20%)
  matrix products  20.5 us (3%)
  local copies, waits for them, and re-layouts  19.3 us (3%)
  between operations  14.2 us (2%)
    unnamed x8, waiting for transfers between devices  218 us
    reduce_scatter x1, waiting for transfers between devices, on_device(): lax.psum_scatter(lax.dot_general(cols, dpre, (((0,), (0,)), ((), ())), pr...  107 us
    all_gather x1, waiting for transfers between devices, on_device(): full_dvel = lax.all_gather(dvel, 'tensor', axis=1, tiled=True)  84.3 us
    all_gather x1, waiting for transfers between devices, on_device(): full_in = lax.all_gather(hidden_input_rows, 'tensor', axis=1, tiled=True)  78.6 us
    psum x1, blocking collectives, on_device(): lax.psum((jnp.sum(normalized_input_gradient, axis=1), jnp.sum(normalized_...  72 us
    psum x1, blocking collectives, on_device(): lax.psum((jnp.sum(input_tokens, axis=1), jnp.sum(input_tokens * input_tok...  68.9 us
    reduce_scatter x1, waiting for transfers between devices, on_device(): lax.psum_scatter(lax.dot_general(cols, act, (((0,), (0,)), ((), ())), pre...  36.7 us
    unnamed x15, local copies, waits for them, and re-layouts  15 us
  transfers between devices with their start and end apart: 6, of which 6 were waited for; matrix products, arithmetic and copies ran while one was open for 2% of the time, Pallas kernels for 0%

commit v1 on v0

v1 whole, which is shorter than its diff:
```python
import functools

import jax
import jax.numpy as jnp
from jax import lax
from jax.experimental import pallas as pl
from jax.experimental.pallas import tpu as pltpu
from jax.sharding import PartitionSpec as P

MESH = pl.DeviceIdType.MESH
BF = jnp.bfloat16
F32 = jnp.float32
NT = (((1,), (1,)), ((), ()))
ORDER = (4, 3, -3, 2, -2, 1, -1, 0)
N_COPIES = 136


def hops(lane, way):
    return 4 if (lane == 0) == (way == 1) else 3


def dot(a, b):
    return jnp.dot(a, b, preferred_element_type=F32)


def block_kernel(
    width,
    x_ref,
    cot_ref,
    mod_ref,
    down_hbm,
    up_hbm,
    mixed_ref,
    tok_ref,
    gd_ref,
    gu_ref,
    W,
    WT,
    G,
    GP,
    ST,
    SZ,
    XH,
    DA,
    AD,
    ADP,
    VS,
    R1,
    PT,
    SB,
    RB,
    XS,
    XR,
    GS,
    GR,
    send_sem,
    recv_sem,
    w_sem,
):
    d, t = lax.axis_index("dp"), lax.axis_index("tensor")
    z, xh, c = t // 4, (t // 2) % 2, t % 2
    y, xl = d // 2, d % 2
    rows, tokens = x_ref.shape
    hidden = W.shape[-1]

    def at(zz, hi, core):
        return (d, zz * 4 + hi * 2 + core)

    def zoff(off):
        return lax.rem(z + off % 8, 8)

    sibling = at(z, xh, 1 - c)
    xpart = at(z, 1 - xh, c)
    xcross = at(z, 1 - xh, 1 - c)
    zpeers = [at(zoff(k), xh, c) for k in range(1, 8)]
    xlo = (y * 2 + 1 - xl, t)
    ypeers = [(lax.rem(y + j, 4) * 2 + xl, t) for j in range(1, 4)]
    local = [sibling, xpart, xcross]

    flight = {}

    def send(key, src, dst, device):
        n = len(flight)
        copy = pltpu.make_async_remote_copy(
            src_ref=src,
            dst_ref=dst,
            send_sem=send_sem.at[n],
            recv_sem=recv_sem.at[n],
            device_id=device,
            device_id_type=MESH,
        )
        copy.start()
        flight[key] = copy

    def arrived(*key):
        flight[key].wait_recv()

    w_copies = [
        pltpu.make_async_copy(down_hbm, W.at[0], w_sem.at[0]),
        pltpu.make_async_copy(up_hbm, W.at[1], w_sem.at[1]),
    ]
    for copy in w_copies:
        copy.start()
    barrier = pltpu.get_barrier_semaphore()
    peers = local + zpeers + [xlo] + ypeers
    for peer in peers:
        pl.semaphore_signal(barrier, inc=1, device_id=peer, device_id_type=MESH)

    def block(a, zz, col):
        return G.at[a, zz // 2, zz % 2, col, c]

    def pair(a, zz):
        return G.at[a, zz // 2, zz % 2, :, c]

    def lane_col(lane):
        return xh if lane == 0 else 1 - xh

    def ring(a, lane, way, step, zz):
        ref = block(a, zz, lane_col(lane))
        send(("ring", a, lane, way, step), ref, ref, at(zoff(way), xh, c))

    def to_sibling(a, off):
        ref = pair(a, zoff(off))
        send(("sib", a, off % 8), ref, ref, sibling)

    def gather_start(a):
        ref = block(a, z, xh)
        send(("agx", a), ref, ref, xpart)
        for way in (1, -1):
            ring(a, 0, way, 1, z)

    def gather_other(a):
        arrived("agx", a)
        for way in (-1, 1):
            ring(a, 1, way, 1, z)
        to_sibling(a, 0)

    def gather_step(a, step):
        for lane in (0, 1):
            for way in (1, -1):
                if hops(lane, way) < step:
                    continue
                arrived("ring", a, lane, way, step)
                if step < hops(lane, way):
                    ring(a, lane, way, step + 1, zoff(-way * step))
        for way in (1, -1) if step < 4 else (1,):
            to_sibling(a, -way * step)

    def gather_end(a):
        for off in range(8):
            arrived("sib", a, off)

    def neighbour_rows(a):
        send(("xlo", a), G.at[a, :, 1 - xl, :, c], GP.at[a, :, :, c], xlo)

    def neighbour_share(a):
        arrived("xlo", a)
        ref = GP.at[a, :, :, c]
        send(("xlosib", a), ref, ref, sibling)

    def sums_local(phase):
        for j, peer in enumerate(local):
            send(("st", phase, j), ST.at[phase, 0], ST.at[phase, j + 1], peer)

    def sums_z(phase):
        for j in range(3):
            arrived("st", phase, j)
        SZ[phase, 0] = (ST[phase, 0] + ST[phase, 1]) + (ST[phase, 2] + ST[phase, 3])
        for j, peer in enumerate(zpeers):
            send(("sz", phase, j), SZ.at[phase, 0], SZ.at[phase, j + 1], peer)

    def sums_end(phase):
        for j in range(7):
            arrived("sz", phase, j)
        return jnp.sum(SZ[phase], axis=0)

    def turn(a):
        w_copies[a].wait()

        def body(i, carry):
            WT[a, i] = W[a, i].reshape(8 * rows, hidden).T
            return carry

        lax.fori_loop(0, 4, body, 0)

    def project(a):
        def body(i, total):
            return total + dot(WT[a, i], G[a, i].reshape(8 * rows, tokens))

        return lax.fori_loop(0, 4, body, jnp.zeros((hidden, tokens), F32))

    def partial(a, off, core):
        zz = zoff(off)
        return dot(W[a, zz // 2, zz % 2, :, core].reshape(2 * rows, hidden), AD[a]).reshape(
            2, rows, tokens
        )

    def scatter_sibling(a):
        for off in ORDER:
            VS[a, off % 8] = partial(a, off, 1 - c).astype(BF)
            send(("rsib", a, off % 8), VS.at[a, off % 8], R1.at[a, off % 8], sibling)

    def scatter_send(a, lane, way, step, value):
        w = (1 - way) // 2
        SB[a, lane, w, step - 1] = value.astype(BF)
        send(
            ("rring", a, lane, way, step),
            SB.at[a, lane, w, step - 1],
            RB.at[a, lane, w, step - 1],
            at(zoff(way), xh, c),
        )

    def scatter_own(a):
        for n, off in enumerate(ORDER):
            mine = partial(a, off, c)
            arrived("rsib", a, off % 8)
            PT[a, off % 8] = mine + R1[a, off % 8].astype(F32)
            if n == 2:
                for lane in (0, 1):
                    for way in (1, -1):
                        first = (way * hops(lane, way)) % 8
                        scatter_send(a, lane, way, 1, PT[a, first, lane_col(lane)])

    def received(a, lane, way, step):
        return RB[a, lane, (1 - way) // 2, step - 1].astype(F32)

    def scatter_step(a, step):
        for lane in (0, 1):
            for way in (1, -1):
                reach = hops(lane, way)
                if reach < step:
                    continue
                arrived("rring", a, lane, way, step)
                if step < reach:
                    off = (way * (reach - step)) % 8
                    value = received(a, lane, way, step) + PT[a, off, lane_col(lane)]
                    scatter_send(a, lane, way, step + 1, value)

    def scatter_total(a, lane):
        total = PT[a, 0, lane_col(lane)]
        for way in (1, -1):
            total = total + received(a, lane, way, hops(lane, way))
        return total

    def scatter_cross(a):
        XS[a] = scatter_total(a, 1).astype(BF)
        send(("rsx", a), XS.at[a], XR.at[a], xpart)

    def scatter_end(a):
        total = scatter_total(a, 0)
        arrived("rsx", a)
        return total + XR[a].astype(F32)

    grad_out = (gd_ref, gu_ref)

    def grad_block(a, j):
        yy = lax.rem(y + j, 4)
        mine = G[a, yy, xl].reshape(4 * rows, tokens)
        theirs = GP[a, yy].reshape(4 * rows, tokens)
        total = lax.dot_general(mine, AD[a], NT, preferred_element_type=F32)
        total = total + lax.dot_general(theirs, ADP[a], NT, preferred_element_type=F32)
        if j == 0:
            grad_out[a][...] = total
        else:
            GS[a, j - 1] = total.astype(BF)
            send(("grad", a, j), GS.at[a, j - 1], GR.at[a, j - 1], ypeers[j - 1])

    def grad_end(a):
        for j in (1, 3, 2):
            arrived("grad", a, j)
        grad_out[a][...] = (
            grad_out[a][...]
            + GR[a, 0].astype(F32)
            + GR[a, 1].astype(F32)
            + GR[a, 2].astype(F32)
        )

    x = x_ref[...].astype(F32)
    ST[0, 0, 0:1, :] = jnp.sum(x, axis=0, keepdims=True)
    ST[0, 0, 1:2, :] = jnp.sum(x * x, axis=0, keepdims=True)
    G[0, z // 2, z % 2, xh, c] = (cot_ref[...].astype(F32) * mod_ref[2]).astype(BF)
    pl.semaphore_wait(barrier, len(peers))
    sums_local(0)
    gather_start(0)
    turn(0)
    sums_z(0)
    gather_other(0)
    gather_step(0, 1)
    sums = sums_end(0)
    mean = sums[0:1, :] / width
    var = sums[1:2, :] / width - mean * mean
    rstd = lax.rsqrt(var + 1e-06)
    xhat = (x_ref[...].astype(F32) - mean) * rstd
    XH[...] = xhat
    G[1, z // 2, z % 2, xh, c] = (xhat * (1.0 + mod_ref[1]) + mod_ref[0]).astype(BF)
    gather_start(1)
    gather_step(0, 2)
    turn(1)
    gather_other(1)
    gather_step(0, 3)
    gather_step(1, 1)
    gather_step(0, 4)
    neighbour_rows(0)
    gather_step(1, 2)
    gather_end(0)
    DA[...] = project(0)
    gather_step(1, 3)
    neighbour_share(0)
    gather_step(1, 4)
    neighbour_rows(1)
    gather_end(1)
    pre = project(1)
    root = 0.7978845608028654
    bend = jnp.tanh(root * (pre + 0.044715 * (pre * pre * pre)))
    AD[0] = (0.5 * pre * (1.0 + bend)).astype(BF)
    send(("ad", 0), AD.at[0], ADP.at[0], xlo)
    slope = 0.5 * (1.0 + bend) + 0.5 * pre * (1.0 - bend * bend) * (
        root * (1.0 + 3.0 * 0.044715 * (pre * pre))
    )
    AD[1] = (DA[...] * slope).astype(BF)
    send(("ad", 1), AD.at[1], ADP.at[1], xlo)
    scatter_sibling(0)
    scatter_own(0)
    scatter_sibling(1)
    scatter_own(1)
    scatter_step(0, 1)
    neighbour_share(1)
    arrived("ad", 0)
    arrived("xlosib", 0)
    grad_block(0, 2)
    scatter_step(1, 1)
    grad_block(0, 1)
    scatter_step(0, 2)
    grad_block(0, 3)
    scatter_step(1, 2)
    arrived("ad", 1)
    arrived("xlosib", 1)
    grad_block(1, 2)
    scatter_step(0, 3)
    grad_block(1, 1)
    scatter_step(1, 3)
    grad_block(1, 3)
    scatter_step(0, 4)
    scatter_cross(0)
    scatter_step(1, 4)
    scatter_cross(1)
    grad_block(0, 0)
    grad_block(1, 0)
    dxhat = scatter_end(1) * (1.0 + mod_ref[1])
    ST[1, 0, 0:1, :] = jnp.sum(dxhat, axis=0, keepdims=True)
    ST[1, 0, 1:2, :] = jnp.sum(dxhat * XH[...], axis=0, keepdims=True)
    sums_local(1)
    velocity = scatter_end(0)
    mixed_ref[...] = (x_ref[...].astype(F32) + mod_ref[2] * velocity).astype(BF)
    sums_z(1)
    grad_end(0)
    sums = sums_end(1)
    tok_ref[...] = (
        cot_ref[...].astype(F32)
        + rstd * (dxhat - sums[0:1, :] / width - XH[...] * (sums[1:2, :] / width))
    ).astype(BF)
    grad_end(1)
    for copy in flight.values():
        copy.wait_send()


def lookup(modulation, buckets):
    n, kinds, cols = modulation.shape
    table = modulation.reshape(n, kinds * cols)
    high = lax.reduce_precision(table, 8, 7)
    rest = table - high
    middle = lax.reduce_precision(rest, 8, 7)
    low = rest - middle
    chosen = (lax.broadcasted_iota(jnp.int32, (n, buckets.shape[0]), 0) == buckets[None, :]).astype(BF)
    pieces = [
        lax.dot_general(
            piece.astype(BF), chosen, (((0,), (0,)), ((), ())), preferred_element_type=F32
        )
        for piece in (high, middle, low)
    ]
    return (pieces[0] + pieces[1] + pieces[2]).reshape(kinds, cols, buckets.shape[0])


def on_device(tokens, buckets, modulation, up_weight, down_weight, output_cotangent):
    batch, rows = tokens.shape
    hidden = up_weight.shape[1]
    groups = lax.axis_size("tensor")
    width = rows * groups
    shape5 = (4, 2, 2, 2, rows, hidden)
    cond = lookup(modulation, buckets)
    vmem = pl.BlockSpec(memory_space=pltpu.VMEM)
    anyspace = pl.BlockSpec(memory_space=pl.ANY)
    V = pltpu.VMEM
    mixed, tok, grad_down, grad_up = pl.pallas_call(
        functools.partial(block_kernel, width),
        out_shape=(
            jax.ShapeDtypeStruct((rows, batch), BF),
            jax.ShapeDtypeStruct((rows, batch), BF),
            jax.ShapeDtypeStruct((4 * rows, hidden), F32),
            jax.ShapeDtypeStruct((4 * rows, hidden), F32),
        ),
        in_specs=[vmem, vmem, vmem, anyspace, anyspace],
        out_specs=(vmem,) * 4,
        scratch_shapes=[
            V((2,) + shape5, BF),
            V((2, 4, hidden, 8 * rows), BF),
            V((2, 4, 2, 2, 2, rows, batch), BF),
            V((2, 4, 2, 2, rows, batch), BF),
            V((2, 4, 2, batch), F32),
            V((2, 8, 2, batch), F32),
            V((rows, batch), F32),
            V((hidden, batch), F32),
            V((2, hidden, batch), BF),
            V((2, hidden, batch), BF),
            V((2, 8, 2, rows, batch), BF),
            V((2, 8, 2, rows, batch), BF),
            V((2, 8, 2, rows, batch), F32),
            V((2, 2, 2, 4, rows, batch), BF),
            V((2, 2, 2, 4, rows, batch), BF),
            V((2, rows, batch), BF),
            V((2, rows, batch), BF),
            V((2, 3, 4 * rows, hidden), BF),
            V((2, 3, 4 * rows, hidden), BF),
            pltpu.SemaphoreType.DMA((N_COPIES,)),
            pltpu.SemaphoreType.DMA((N_COPIES,)),
            pltpu.SemaphoreType.DMA((2,)),
        ],
        compiler_params=pltpu.CompilerParams(
            collective_id=0, has_side_effects=True, vmem_limit_bytes=56 * 1024 * 1024
        ),
        name="mlp_block",
    )(
        tokens.T,
        output_cotangent.T,
        cond,
        down_weight.reshape(shape5),
        up_weight.reshape(shape5),
    )
    return mixed.T, tok.T, grad_up, grad_down


def solution(mesh):
    placed = (
        P("dp", "tensor"),
        P("dp"),
        P(None, None, "tensor"),
        P(None, "tensor"),
        P(None, "tensor"),
        P("dp", "tensor"),
    )
    return jax.shard_map(
        on_device,
        mesh=mesh,
        in_specs=placed,
        out_specs=(P("dp", "tensor"), P("dp", "tensor"), P("dp", "tensor"), P("dp", "tensor")),
        check_vma=False,
    )
```

time: 723 us -> 91.9 us (0.13)
  waiting for transfers between devices: 524 us -> 0 us
  blocking collectives: 141 us -> 0 us
  Pallas kernels: 0 us -> 81.8 us
  matrix products: 20.5 us -> 1.89 us
  local copies, waits for them, and re-layouts: 19.3 us -> 5.64 us
  between operations: 14.2 us -> 0.69 us
    unnamed x8 -> x0, waiting for transfers between devices: 218 us -> none
    all_gather x2 -> x0, waiting for transfers between devices: 163 us -> none  [the longest x1 84.3 us: on_device(): full_dvel = lax.all_gather(dvel, 'tensor', axis=1, tiled=True)]
    reduce_scatter x2 -> x0, waiting for transfers between devices: 143 us -> none  [the longest x1 107 us: on_device(): lax.psum_scatter(lax.dot_general(cols, dpre, (((0,), (0,)), ((), ())), pr...]
    psum x2 -> x0, blocking collectives: 141 us -> none  [the longest x1 72 us: on_device(): lax.psum((jnp.sum(normalized_input_gradient, axis=1), jnp.sum(normalized_...]
    pallas_call x0 -> x1, Pallas kernels: none -> 81.8 us  [on_device(): pl.pallas_call(functools.partial(block_kernel, width), out_shape=(jax.Sha...]
    dot_general x6 -> x3, matrix products: 20.5 us -> 1.89 us  [lookup(): lax.dot_general(piece.astype(BF), chosen, (((0,), (0,)), ((), ())), prefe...]
    unnamed x15 -> x8, local copies, waits for them, and re-layouts: 15 us -> 5.64 us
  transfers between devices with their start and end apart: 6 -> 0, of which waited for: 6 -> 0; matrix products, arithmetic and copies ran while one was open for 2% -> 0% of each run, Pallas kernels for 0% -> 0%
where the time goes in v1:
time: 91.9 us; the launch traced here: 91.6 us
  Pallas kernels  81.8 us (89%)
  local copies, waits for them, and re-layouts  5.64 us (6%)
  matrix products  1.89 us (2%)
  other arithmetic  1.61 us (2%)
    pallas_call x1, Pallas kernels, on_device(): pl.pallas_call(functools.partial(block_kernel, width), out_shape=(jax.Sha...  81.8 us
    unnamed x8, local copies, waits for them, and re-layouts  5.64 us
    dot_general x3, matrix products, lookup(): lax.dot_general(piece.astype(BF), chosen, (((0,), (0,)), ((), ())), prefe...  1.89 us

profile of v1, /device:TPU:1, one launch (start us, length us, event | category | flops | bytes accessed | tf_op | source)
XLA Modules:
  0.0 91.6 jit_solution(10902473452678000755)
XLA Ops:
  0.6 0.0 copy-start.1
  0.6 1.6 %fusion = (bf16[1000,288]{0,1:T(8,128)(2,1)S(1)}, bf16[1000,288]{0,1:T(8,128)(2,1)S(1)}, bf16[1000,288]{0,1:T(8,128)(2,1)S(1)}) fusion(f32[1000,3,96]{0,2,1:T(8,128)} %param.8), kind=kLoop, calls=%fused_computation.4 | loop fusion | flops 2016000 | bytes 2880000 | tf_op jit(solution)/shard_map/convert_element_type | solution.py:377
  2.3 0.0 copy-done.1
  2.3 0.4 convolution_bitcast_fusion
  2.7 0.4 convolution_add_fusion.1
  3.1 1.1 %convolution_add_fusion = f32[288,256]{1,0:T(8,128)} fusion(f32[288,256]{1,0:T(8,128)S(1)} %convolution_add_fusion.1, bf16[1000,288]{0,1:T(8,128)(2,1)S(1)} %get-tuple-element.12, s32[256]{0:T(256)S(1)} %copy-done.1), kind=kOutput, calls=%fused_computation.5 | convolution fusion | flops 147785728 | bytes 1166848 | tf_op jit(solution)/shard_map/dot_general | solution.py:376
  4.2 81.8 %mlp_block.1 = (bf16[96,256]{1,0:T(8,128)(2,1)}, bf16[96,256]{1,0:T(8,128)(2,1)}, f32[384,384]{1,0:T(8,128)}, f32[384,384]{1,0:T(8,128)}) custom-call(bf16[96,256]{1,0:T(8,128)(2,1)} %bitcast.22, bf16[96,256]{1,0:T(8,128)(2,1)} %bitcast.23, f32[3,96,256]{2,1,0:T(8,128)} %bitcast.21, bf16[4,2,2,2,96,384]{5,4,3,2,1,0:T(8,128)(2,1)} %bitcast.19, ...), custom_call_target="tpu_custom_call" | custom-call | tf_op jit(solution)/shard_map/mlp_block/pallas_call | solution.py:394
  86.0 0.0 copy-start
  86.0 1.5 %copy.14 = bf16[256,96]{0,1:T(8,128)(2,1)} copy(bf16[256,96]{0,1:T(8,128)(2,1)} %bitcast.25) | data formatting | bytes 98304
  87.5 1.4 %copy.15 = bf16[256,96]{0,1:T(8,128)(2,1)} copy(bf16[256,96]{0,1:T(8,128)(2,1)} %bitcast.24) | data formatting | bytes 98304
  88.9 1.9 %copy.16 = f32[384,384]{1,0:T(8,128)} copy(f32[384,384]{1,0:T(8,128)} %get-tuple-element.21) | data formatting | bytes 1179648
  90.8 0.0 copy-done
  90.8 0.8 copy.17
Async XLA Ops:
  0.6 1.6 %copy-start.1 = (s32[256]{0:T(256)S(1)}, s32[256]{0:T(256)}, u32[]{:S(2)}) copy-start(s32[256]{0:T(256)} %param.7) | copy-start | bytes 3076
  86.0 4.8 %copy-start = (f32[384,384]{1,0:T(8,128)S(1)}, f32[384,384]{1,0:T(8,128)}, u32[]{:S(2)}) copy-start(f32[384,384]{1,0:T(8,128)} %get-tuple-element.22) | copy-start | bytes 1769476

commit v2 on v1

v2 whole, which is shorter than its diff:
```python
import functools

import jax
import jax.numpy as jnp
from jax import lax
from jax.experimental import pallas as pl
from jax.experimental.pallas import tpu as pltpu
from jax.sharding import PartitionSpec as P

MESH = pl.DeviceIdType.MESH
BF = jnp.bfloat16
F32 = jnp.float32
NT = (((1,), (1,)), ((), ()))
FIRST = (4, 3, -3)
REST = (2, -2, 1, -1, 0)
SENDS, RECEIVES = 75, 103


def hops(lane, way):
    return 4 if (lane == 0) == (way == 1) else 3


def dot(a, b):
    return jnp.dot(a, b, preferred_element_type=F32)


def block_kernel(
    width,
    x_hbm,
    cot_hbm,
    buckets_hbm,
    table_hbm,
    down_hbm,
    up_hbm,
    mixed_ref,
    tok_ref,
    gd_ref,
    gu_ref,
    x_ref,
    cot_ref,
    bucket_ref,
    table_ref,
    mod_ref,
    W,
    WT,
    G,
    GP,
    ST,
    SZ,
    SA,
    XH,
    DA,
    AD,
    ADP,
    VS,
    R1,
    PT,
    SB,
    RB,
    XS,
    XR,
    GS,
    GH,
    GR,
    send_sem,
    recv_sem,
    w_sem,
):
    d, t = lax.axis_index("dp"), lax.axis_index("tensor")
    z, xh, c = t // 4, (t // 2) % 2, t % 2
    y, xl = d // 2, d % 2
    rows, tokens = x_ref.shape
    hidden = W.shape[-1]

    def at(zz, hi, core):
        return (d, zz * 4 + hi * 2 + core)

    def zoff(off):
        return lax.rem(z + off % 8, 8)

    sibling = at(z, xh, 1 - c)
    xpart = at(z, 1 - xh, c)
    xcross = at(z, 1 - xh, 1 - c)
    zpeers = [at(zoff(k), xh, c) for k in range(1, 8)]
    xlo = (y * 2 + 1 - xl, t)
    ypeers = [(lax.rem(y + j, 4) * 2 + xl, t) for j in range(1, 4)]
    local = [sibling, xpart, xcross]

    flight, slots = {}, {}
    used = [0, 0]

    def make(src, dst, device, pair):
        return pltpu.make_async_remote_copy(
            src_ref=src,
            dst_ref=dst,
            send_sem=send_sem.at[pair[0]],
            recv_sem=recv_sem.at[pair[1]],
            device_id=device,
            device_id_type=MESH,
        )

    def new_pair(after=None):
        if after is None:
            first, used[0] = used[0], used[0] + 1
        else:
            flight.pop(after).wait_send()
            first = slots[after][0]
        used[1] += 1
        return first, used[1] - 1

    def send(key, src, dst, device, after=None):
        slots[key] = new_pair(after)
        flight[key] = make(src, dst, device, slots[key])
        flight[key].start()

    def send_in(group, total_src, total_dst, src, dst, device):
        if group not in slots:
            slots[group] = new_pair()
            flight[group] = make(total_src, total_dst, device, slots[group])
        make(src, dst, device, slots[group]).start()

    def arrived(*key):
        flight[key].wait_recv()

    barrier = pltpu.get_barrier_semaphore()
    peers = zpeers + local + [xlo] + ypeers
    for peer in peers:
        pl.semaphore_signal(barrier, inc=1, device_id=peer, device_id_type=MESH)
    in_copies = [
        pltpu.make_async_copy(src, dst, w_sem.at[n])
        for n, (src, dst) in enumerate(
            (
                (x_hbm, x_ref),
                (cot_hbm, cot_ref),
                (buckets_hbm, bucket_ref),
                (table_hbm, table_ref),
                (down_hbm, W.at[0]),
                (up_hbm, W.at[1]),
            )
        )
    ]
    for copy in in_copies:
        copy.start()

    def block(a, zz, col):
        return G.at[a, zz // 2, zz % 2, col, c]

    def pair(a, zz):
        return G.at[a, zz // 2, zz % 2, :, c]

    def lane_col(lane):
        return xh if lane == 0 else 1 - xh

    def ring(a, lane, way, step, zz):
        ref = block(a, zz, lane_col(lane))
        send(("ring", a, lane, way, step), ref, ref, at(zoff(way), xh, c))

    def to_sibling(a, off):
        ref = pair(a, zoff(off))
        send_in(
            ("sib", a), G.at[a, :, :, :, c], G.at[a, :, :, :, 1 - c], ref, ref, sibling
        )

    def gather_start(a):
        ref = block(a, z, xh)
        send(("agx", a), ref, ref, xpart)
        for way in (1, -1):
            ring(a, 0, way, 1, z)

    def gather_other(a):
        arrived("agx", a)
        for way in (-1, 1):
            ring(a, 1, way, 1, z)
        to_sibling(a, 0)

    def gather_step(a, lane, step):
        for way in (1, -1) if lane == 0 else (-1, 1):
            if hops(lane, way) < step:
                continue
            arrived("ring", a, lane, way, step)
            if step < hops(lane, way):
                ring(a, lane, way, step + 1, zoff(-way * step))
        if lane == 1:
            for way in (1, -1) if step < 4 else (1,):
                to_sibling(a, -way * step)

    def gather_end(a):
        arrived("sib", a)

    odd = lax.rem(z + 1 - xl, 2)
    far = (odd, 2 - 3 * odd, 5 * odd - 2, 4 - 7 * odd)

    def neighbour_rows(a, half):
        for n in (2 * half, 2 * half + 1):
            zz = lax.rem(z + far[n] + 8, 8)
            send_in(
                ("xlo", a),
                G.at[a, :, 1 - xl, :, c],
                GP.at[a, :, :, c],
                G.at[a, zz // 2, zz % 2, :, c],
                GP.at[a, zz // 2, :, c],
                xlo,
            )

    def neighbour_share(a):
        arrived("xlo", a)
        ref = GP.at[a, :, :, c]
        send(("xlosib", a), ref, ref, sibling)

    def sums_local():
        for j, peer in enumerate(local):
            send(("st", j), ST.at[0], ST.at[j + 1], peer)

    def sums_z():
        for j in range(3):
            arrived("st", j)
        SZ[0] = (ST[0] + ST[1]) + (ST[2] + ST[3])
        for j, peer in enumerate(zpeers):
            send(("sz", j), SZ.at[0], SZ.at[j + 1], peer)

    def sums_end():
        for j in range(7):
            arrived("sz", j)
        return jnp.sum(SZ[...], axis=0)

    def sums_all():
        for n in range(31, 0, -1):
            k, hi, core = n // 4, (n // 2) % 2, n % 2
            peer = at(zoff(k), xh if hi == 0 else 1 - xh, c if core == 0 else 1 - c)
            send_in(("sa",), SA.at[1:32], SA.at[1:32], SA.at[0], SA.at[n], peer)

    def sums_all_end():
        arrived("sa")
        return jnp.sum(SA[...], axis=0)

    def turn(a):
        in_copies[4 + a].wait()

        def body(i, carry):
            WT[a, i] = W[a, i].reshape(8 * rows, hidden).T
            return carry

        lax.fori_loop(0, 4, body, 0)

    def project(a):
        def body(i, total):
            return total + dot(WT[a, i], G[a, i].reshape(8 * rows, tokens))

        return lax.fori_loop(0, 4, body, jnp.zeros((hidden, tokens), F32))

    def partial(a, off, core):
        zz = zoff(off)
        return dot(W[a, zz // 2, zz % 2, :, core].reshape(2 * rows, hidden), AD[a]).reshape(
            2, rows, tokens
        )

    def scatter_sibling(a, offsets):
        for off in offsets:
            VS[a, off % 8] = partial(a, off, 1 - c).astype(BF)
            send(("rsib", a, off % 8), VS.at[a, off % 8], R1.at[a, off % 8], sibling)

    def scatter_send(a, lane, way, step, value):
        w = (1 - way) // 2
        SB[a, lane, w, step - 1] = value.astype(BF)
        send(
            ("rring", a, lane, way, step),
            SB.at[a, lane, w, step - 1],
            RB.at[a, lane, w, step - 1],
            at(zoff(way), xh, c),
            after=("ring", a, lane, way, step),
        )

    def scatter_own(a, offsets):
        for off in offsets:
            mine = partial(a, off, c)
            arrived("rsib", a, off % 8)
            PT[a, off % 8] = mine + R1[a, off % 8].astype(F32)

    def scatter_start(a):
        scatter_own(a, FIRST)
        for lane in (0, 1):
            for way in (1, -1):
                first = (way * hops(lane, way)) % 8
                scatter_send(a, lane, way, 1, PT[a, first, lane_col(lane)])

    def received(a, lane, way, step):
        return RB[a, lane, (1 - way) // 2, step - 1].astype(F32)

    def scatter_step(a, step):
        for lane in (0, 1):
            for way in (1, -1):
                reach = hops(lane, way)
                if reach < step:
                    continue
                arrived("rring", a, lane, way, step)
                if step < reach:
                    off = (way * (reach - step)) % 8
                    value = received(a, lane, way, step) + PT[a, off, lane_col(lane)]
                    scatter_send(a, lane, way, step + 1, value)

    def scatter_total(a, lane):
        total = PT[a, 0, lane_col(lane)]
        for way in (1, -1):
            total = total + received(a, lane, way, hops(lane, way))
        return total

    def scatter_cross(a):
        XS[a] = scatter_total(a, 1).astype(BF)
        send(("rsx", a), XS.at[a], XR.at[a], xpart)

    def scatter_end(a):
        total = scatter_total(a, 0)
        arrived("rsx", a)
        return total + XR[a].astype(F32)

    grad_out = (gd_ref, gu_ref)

    half = 2 * rows

    def grad_total(a, j):
        yy = lax.rem(y + j, 4)
        mine = G[a, yy, xl].reshape(4 * rows, tokens)
        theirs = GP[a, yy].reshape(4 * rows, tokens)
        total = lax.dot_general(mine, AD[a], NT, preferred_element_type=F32)
        return total + lax.dot_general(theirs, ADP[a], NT, preferred_element_type=F32)

    def grad_far(a):
        GS[a, 0] = grad_total(a, 2).astype(BF)
        for w, peer in enumerate((ypeers[0], ypeers[2])):
            part = GS.at[a, 0, w * half : (w + 1) * half]
            send(("far", a, w), part, GH.at[a, w], peer)

    def grad_near(a):
        total = grad_total(a, 1)
        arrived("far", a, 0)
        GS[a, 1, :half] = (total[:half] + GH[a, 0].astype(F32)).astype(BF)
        GS[a, 1, half:] = total[half:].astype(BF)
        send(("grad", a, 0), GS.at[a, 1], GR.at[a, 0], ypeers[0])
        total = grad_total(a, 3)
        arrived("far", a, 1)
        GS[a, 2, :half] = total[:half].astype(BF)
        GS[a, 2, half:] = (total[half:] + GH[a, 1].astype(F32)).astype(BF)
        send(("grad", a, 1), GS.at[a, 2], GR.at[a, 1], ypeers[2])

    def grad_own(a):
        grad_out[a][...] = grad_total(a, 0)

    def grad_end(a):
        for w in range(2):
            arrived("grad", a, w)
        grad_out[a][...] = grad_out[a][...] + GR[a, 0].astype(F32) + GR[a, 1].astype(F32)

    def lookup(kind, chosen):
        table = table_ref[kind]
        high = table.astype(BF)
        rest = table - high.astype(F32)
        middle = rest.astype(BF)
        low = (rest - middle.astype(F32)).astype(BF)
        mod_ref[kind] = (dot(high, chosen) + dot(middle, chosen)) + dot(low, chosen)

    def begin():
        for n in range(4):
            in_copies[n].wait()
        x = x_ref[...].astype(F32)
        ST[0, 0:1, :] = jnp.sum(x, axis=0, keepdims=True)
        ST[0, 1:2, :] = jnp.sum(x * x, axis=0, keepdims=True)
        here = lax.broadcasted_iota(jnp.int32, (table_ref.shape[2], tokens), 0)
        chosen = (here == bucket_ref[...]).astype(F32).astype(BF)
        lookup(2, chosen)
        G[0, z // 2, z % 2, xh, c] = (cot_ref[...].astype(F32) * mod_ref[2]).astype(BF)
        lookup(0, chosen)
        lookup(1, chosen)

    begin()
    pl.semaphore_wait(barrier, len(peers))
    sums_local()
    gather_start(0)
    turn(0)
    turn(1)
    gather_step(0, 0, 1)
    sums_z()
    gather_other(0)
    gather_step(0, 0, 2)
    gather_step(0, 1, 1)
    sums = sums_end()
    mean = sums[0:1, :] / width
    var = sums[1:2, :] / width - mean * mean
    rstd = lax.rsqrt(var + 1e-06)
    xhat = (x_ref[...].astype(F32) - mean) * rstd
    XH[...] = xhat
    G[1, z // 2, z % 2, xh, c] = (xhat * (1.0 + mod_ref[1]) + mod_ref[0]).astype(BF)
    gather_start(1)
    gather_step(0, 0, 3)
    gather_step(0, 1, 2)
    neighbour_rows(0, 0)
    gather_step(1, 0, 1)
    gather_step(0, 0, 4)
    gather_other(1)
    gather_step(0, 1, 3)
    gather_step(1, 0, 2)
    gather_step(1, 1, 1)
    gather_step(0, 1, 4)
    neighbour_rows(0, 1)
    gather_step(1, 0, 3)
    gather_step(1, 1, 2)
    neighbour_rows(1, 0)
    gather_end(0)
    DA[...] = project(0)
    gather_step(1, 0, 4)
    gather_step(1, 1, 3)
    neighbour_share(0)
    gather_step(1, 1, 4)
    gather_end(1)
    pre = project(1)
    root = 0.7978845608028654
    bend = jnp.tanh(root * (pre + 0.044715 * (pre * pre * pre)))
    AD[0] = (0.5 * pre * (1.0 + bend)).astype(BF)
    send(("ad", 0), AD.at[0], ADP.at[0], xlo)
    neighbour_rows(1, 1)
    slope = 0.5 * (1.0 + bend) + 0.5 * pre * (1.0 - bend * bend) * (
        root * (1.0 + 3.0 * 0.044715 * (pre * pre))
    )
    AD[1] = (DA[...] * slope).astype(BF)
    send(("ad", 1), AD.at[1], ADP.at[1], xlo)
    scatter_sibling(1, FIRST)
    scatter_sibling(1, REST)
    scatter_start(1)
    scatter_own(1, REST)
    scatter_sibling(0, FIRST)
    scatter_sibling(0, REST)
    scatter_step(1, 1)
    arrived("xlosib", 0)
    arrived("ad", 0)
    grad_far(0)
    scatter_start(0)
    scatter_step(1, 2)
    scatter_own(0, REST)
    scatter_step(0, 1)
    grad_near(0)
    scatter_step(1, 3)
    neighbour_share(1)
    scatter_step(0, 2)
    arrived("ad", 1)
    arrived("xlosib", 1)
    grad_far(1)
    scatter_step(1, 4)
    scatter_cross(1)
    scatter_step(0, 3)
    grad_own(0)
    grad_own(1)
    dxhat = scatter_end(1) * (1.0 + mod_ref[1])
    SA[0, 0:1, :] = jnp.sum(dxhat, axis=0, keepdims=True)
    SA[0, 1:2, :] = jnp.sum(dxhat * XH[...], axis=0, keepdims=True)
    sums_all()
    grad_near(1)
    scatter_step(0, 4)
    scatter_cross(0)
    velocity = scatter_end(0)
    mixed_ref[...] = (x_ref[...].astype(F32) + mod_ref[2] * velocity).astype(BF)
    grad_end(0)
    sums = sums_all_end()
    tok_ref[...] = (
        cot_ref[...].astype(F32)
        + rstd * (dxhat - sums[0:1, :] / width - XH[...] * (sums[1:2, :] / width))
    ).astype(BF)
    grad_end(1)

    def finish():
        for copy in flight.values():
            copy.wait_send()

    finish()
    assert used == [SENDS, RECEIVES], used


def on_device(tokens, buckets, modulation, up_weight, down_weight, output_cotangent):
    batch, rows = tokens.shape
    hidden = up_weight.shape[1]
    groups = lax.axis_size("tensor")
    width = rows * groups
    shape5 = (4, 2, 2, 2, rows, hidden)
    table = jnp.transpose(modulation, (1, 2, 0))
    vmem = pl.BlockSpec(memory_space=pltpu.VMEM)
    hbm = pl.BlockSpec(memory_space=pltpu.HBM)
    V = pltpu.VMEM
    mixed, tok, grad_down, grad_up = pl.pallas_call(
        functools.partial(block_kernel, width),
        out_shape=(
            V((rows, batch), BF),
            V((rows, batch), BF),
            V((4 * rows, hidden), F32),
            V((4 * rows, hidden), F32),
        ),
        in_specs=[hbm] * 6,
        out_specs=(vmem,) * 4,
        scratch_shapes=[
            V((rows, batch), BF),
            V((rows, batch), BF),
            V((1, batch), jnp.int32),
            V(table.shape, F32),
            V((3, rows, batch), F32),
            V((2,) + shape5, BF),
            V((2, 4, hidden, 8 * rows), BF),
            V((2, 4, 2, 2, 2, rows, batch), BF),
            V((2, 4, 2, 2, rows, batch), BF),
            V((4, 2, batch), F32),
            V((8, 2, batch), F32),
            V((32, 2, batch), F32),
            V((rows, batch), F32),
            V((hidden, batch), F32),
            V((2, hidden, batch), BF),
            V((2, hidden, batch), BF),
            V((2, 8, 2, rows, batch), BF),
            V((2, 8, 2, rows, batch), BF),
            V((2, 8, 2, rows, batch), F32),
            V((2, 2, 2, 4, rows, batch), BF),
            V((2, 2, 2, 4, rows, batch), BF),
            V((2, rows, batch), BF),
            V((2, rows, batch), BF),
            V((2, 3, 4 * rows, hidden), BF),
            V((2, 2, 2 * rows, hidden), BF),
            V((2, 2, 4 * rows, hidden), BF),
            pltpu.SemaphoreType.DMA((SENDS,)),
            pltpu.SemaphoreType.DMA((RECEIVES,)),
            pltpu.SemaphoreType.DMA((6,)),
        ],
        compiler_params=pltpu.CompilerParams(
            collective_id=0, has_side_effects=True, vmem_limit_bytes=36 * 1024 * 1024
        ),
        name="mlp_block",
    )(
        *(
            pltpu.with_memory_space_constraint(v, pltpu.HBM)
            for v in (
                tokens.T,
                output_cotangent.T,
                buckets.reshape(1, batch),
                table,
                down_weight.reshape(shape5),
                up_weight.reshape(shape5),
            )
        )
    )
    return mixed.T, tok.T, grad_up, grad_down


def solution(mesh):
    placed = (
        P("dp", "tensor"),
        P("dp"),
        P(None, None, "tensor"),
        P(None, "tensor"),
        P(None, "tensor"),
        P("dp", "tensor"),
    )
    return jax.shard_map(
        on_device,
        mesh=mesh,
        in_specs=placed,
        out_specs=(P("dp", "tensor"), P("dp", "tensor"), P("dp", "tensor"), P("dp", "tensor")),
        check_vma=False,
    )
```

time: 91.9 us -> 77.1 us (0.84)
  Pallas kernels: 81.8 us -> 73.4 us
  local copies, waits for them, and re-layouts: 5.64 us -> 2.87 us
  matrix products: 1.89 us -> 0 us
  other arithmetic: 1.61 us -> 0 us
    pallas_call x1, Pallas kernels: 81.8 us -> 73.4 us  [on_device(): pl.pallas_call(functools.partial(block_kernel, width), out_shape=(V((rows...]
    unnamed x8 -> x4, local copies, waits for them, and re-layouts: 5.64 us -> 2.87 us
    dot_general x3 -> x0, matrix products: 1.89 us -> none  [lookup(): lax.dot_general(piece.astype(BF), chosen, (((0,), (0,)), ((), ())), prefe...]
    convert_element_type x1 -> x0, other arithmetic: 1.61 us -> none  [lookup(): piece.astype(BF)]
where the time goes in v2:
time: 77.1 us; the launch traced here: 76.9 us
  Pallas kernels  73.4 us (95%)
  local copies, waits for them, and re-layouts  2.87 us (4%)
    pallas_call x1, Pallas kernels, on_device(): pl.pallas_call(functools.partial(block_kernel, width), out_shape=(V((rows...  73.4 us
    unnamed x4, local copies, waits for them, and re-layouts  2.87 us

profile of v2, /device:TPU:1, one launch (start us, length us, event | category | flops | bytes accessed | tf_op | source)
XLA Modules:
  0.0 76.9 jit_solution(1550310135070223347)
XLA Ops:
  0.6 73.4 %mlp_block.1 = (bf16[96,256]{1,0:T(8,128)(2,1)S(1)}, bf16[96,256]{1,0:T(8,128)(2,1)S(1)}, f32[384,384]{1,0:T(8,128)S(1)}, f32[384,384]{1,0:T(8,128)S(1)}) custom-call(bf16[96,256]{1,0:T(8,128)(2,1)} %bitcast.13, bf16[96,256]{1,0:T(8,128)(2,1)} %bitcast.14, s32[1,256]{1,0:T(1,128)} %bitcast.15, f32[3,96,1000]{2,1,0:T(8,128)} %bitcast.12, ...), custom_call_target="tpu_custom_call" | custom-call | tf_op jit(solution)/shard_map/mlp_block/pallas_call | solution.py:486
  74.0 0.6 copy.14
  74.7 0.6 copy.15
  75.3 0.8 %copy.16 = f32[384,384]{1,0:T(8,128)} copy(f32[384,384]{1,0:T(8,128)S(1)} %get-tuple-element.14) | data formatting | bytes 1179648
  76.1 0.8 %copy.17 = f32[384,384]{1,0:T(8,128)} copy(f32[384,384]{1,0:T(8,128)S(1)} %get-tuple-element.15) | data formatting | bytes 1179648
